TPU v7x, 256 devices: a whole 4x4x8 slice. The times are simulated.
256 devices in a mesh: row: 8 (over z_hi, core), col: 32 (over y, x, z_lo).
Axes of the slice: x: 4, y: 4, z: 8 (z_hi: 4, z_lo: 2; z = z_hi * 2 + z_lo), core: 2. Of those that a mesh axis runs over, the one named last changes fastest.
Arguments:
- features: bfloat16 [65536, 256], P(('row', 'col')), may hold values from -6 to 6
- layer_weight: bfloat16 [256, 256], replicated, may hold values from -0.375 to 0.375
- layer_bias: float32 [256], replicated, may hold values from -3 to 3
- cotangent: bfloat16 [65536, 256], P(('row', 'col')), may hold values from -6 to 6
- tile_values: bfloat16 [8192, 256, 256], P(('row', 'col')), may hold values from -0.0625 to 0.0625
- tile_index: int32 [8192, 2], P(('row', 'col')), may hold values from -1 to 255, as said below
Outputs:
- activations: bfloat16 [65536, 256], P(('row', 'col'))
- node_grad: bfloat16 [65536, 256], P(('row', 'col'))
- weight_grad: float32 [256, 256], P(('row', 'col'))
- bias_grad: float32 [256], P(('row', 'col'))
Inputs may be any that keep to these rules, and one draw needn't show every extreme that they name: `tile_index`: each pair is (I, J) with I <= J; device r * 32 + c holds only pairs whose I lies in blocks r * 32 * 1 to (r + 1) * 32 - 1 and whose J // 1 equals c modulo 32. Each pair is held by at most one slot among all devices. A device's live slots come first, its empty slots hold -1 in both entries; counts differ from device to device, and some device fills all 32 slots.
All inputs are finite; a program needn't handle non-finite values.
Results may differ from a plain program's by a relative error of at most 0.025.
Values may be sent and summed in bfloat16 or wider, within the bound.
No kernel may reach another device: no remote copies, remote signals or barrier semaphores. Data moves between devices by JAX's collectives and lax.ppermute only.
A program may use at most 128 MiB of HBM per device.

v0:
```python
import jax
import jax.numpy as jnp
from jax import lax
from jax.sharding import Mesh
from jax.sharding import PartitionSpec as P

BLK_DEV = 1
ROW = ("row_0", "row_1")
ROW_COL = ("row_0", "row_1", "col")


def laid_out(blocks, dim):
    blocks = jnp.moveaxis(blocks, 0, dim)
    shape = blocks.shape
    return blocks.reshape(*shape[:dim], shape[dim] * shape[dim + 1], *shape[dim + 2 :])


def stacked_from(array, axes, sequence):
    blocks = array[None]
    for k in sequence:
        blocks = lax.all_gather(blocks, axes[k], axis=0, tiled=True)
    current = [lax.axis_size(axes[k]) for k in reversed(sequence)]
    blocks = blocks.reshape(*current, *array.shape)
    turned = sorted(range(len(sequence)), key=lambda place: sequence[len(sequence) - 1 - place])
    return blocks.transpose(*turned, *range(len(sequence), blocks.ndim)).reshape(-1, *array.shape)


def gathered_by_axis(array, axes, sequence, dim):
    return laid_out(stacked_from(array, axes, sequence), dim)


def split_up(array, dim, length):
    shape = array.shape
    blocks = array.reshape(*shape[:dim], length, shape[dim] // length, *shape[dim + 1 :])
    return jnp.moveaxis(blocks, dim, 0)


def sent_and_summed(array, axis, dim):
    length = lax.axis_size(axis)
    blocks = lax.all_to_all(split_up(array, dim, length), axis, 0, 0, tiled=True)
    return jnp.sum(blocks.astype(jnp.float32), axis=0)


def sum_in_order(blocks, axes, sequence):
    shape = [lax.axis_size(a) for a in axes]
    blocks = blocks.reshape(*shape, *blocks.shape[1:])
    blocks = blocks.transpose(*sequence, *range(len(axes), blocks.ndim))
    blocks = blocks.reshape(-1, *blocks.shape[len(axes) :])
    for k in sequence:
        blocks = lax.psum_scatter(blocks, axes[k], scatter_dimension=0, tiled=True)
    return blocks[0]


def summed_rows(array, axes, sequence, dim):
    length = lax.axis_size(axes)
    return sum_in_order(split_up(array, dim, length), axes, sequence)


def aggregate(node_data, tile_values, tile_index):
    tile_size = tile_values.shape[1]
    feature_count = node_data.shape[1]
    column_devices = lax.axis_size("col")
    row_index = lax.axis_index(ROW)
    column_group = gathered_by_axis(node_data, ROW, (0, 1), 0)
    row_group = lax.all_gather(node_data, "col", axis=0, tiled=True)
    column_blocks = column_group.reshape(-1, tile_size, feature_count)
    row_blocks = row_group.reshape(-1, tile_size, feature_count)
    row_span = row_blocks.shape[0]
    column_span = column_blocks.shape[0]
    block_row = tile_index[:, 0]
    block_column = tile_index[:, 1]
    occupied = block_row >= 0
    row_slot = jnp.where(occupied, block_row - row_index * row_span, 0)
    column_slot = jnp.where(
        occupied, block_column // BLK_DEV // column_devices * BLK_DEV + block_column % BLK_DEV, 0
    )
    column_inputs = jnp.take(column_blocks, column_slot, axis=0)
    row_inputs = jnp.take(row_blocks, row_slot, axis=0)
    forward_terms = jnp.einsum(
        "tnm,tmf->tnf", tile_values, column_inputs, preferred_element_type=jnp.float32
    )
    mirror_terms = jnp.einsum(
        "tmn,tmf->tnf", tile_values, row_inputs, preferred_element_type=jnp.float32
    )
    live = occupied.astype(jnp.float32)[:, None, None]
    row_partial = (
        jnp.zeros((row_span, tile_size, feature_count), jnp.float32)
        .at[row_slot]
        .add(forward_terms * live)
    )
    column_partial = (
        jnp.zeros((column_span, tile_size, feature_count), jnp.float32)
        .at[column_slot]
        .add(mirror_terms * live)
    )
    row_partial = row_partial.reshape(row_span * tile_size, feature_count)
    column_partial = column_partial.reshape(column_span * tile_size, feature_count)
    row_sums = sent_and_summed(row_partial.astype(jnp.bfloat16), "col", 0)
    column_sums = summed_rows(column_partial.astype(jnp.bfloat16), ROW, (1, 0), 0).astype(
        jnp.float32
    )
    return (row_sums + column_sums).astype(jnp.bfloat16)


def local(features, layer_weight, layer_bias, cotangent, tile_values, tile_index):
    aggregated = aggregate(features, tile_values, tile_index)
    hidden = jnp.dot(aggregated, layer_weight, preferred_element_type=jnp.float32) + layer_bias
    logistic = jax.nn.sigmoid(hidden)
    activations = (hidden * logistic).astype(jnp.bfloat16)
    derivative = logistic * (1.0 + hidden * (1.0 - logistic))
    hidden_grad = (cotangent.astype(jnp.float32) * derivative).astype(jnp.bfloat16)
    message_grad = jnp.dot(hidden_grad, layer_weight.T, preferred_element_type=jnp.float32).astype(
        jnp.bfloat16
    )
    total_nodes = features.shape[0] * lax.axis_size(ROW) * lax.axis_size("col")
    grad_scale = total_nodes ** (-0.5)
    weight_part = (
        lax.dot_general(
            aggregated, hidden_grad, (((0,), (0,)), ((), ())), preferred_element_type=jnp.float32
        )
        * grad_scale
    )
    bias_part = jnp.sum(hidden_grad.astype(jnp.float32), axis=0) * grad_scale
    weight_grad, bias_grad = (
        lax.psum_scatter(weight_part, ROW_COL, scatter_dimension=0, tiled=True),
        lax.psum_scatter(bias_part, ROW_COL, scatter_dimension=0, tiled=True),
    )
    node_grad = aggregate(message_grad, tile_values, tile_index)
    return (activations, node_grad, weight_grad, bias_grad)


def solution(mesh):
    split = Mesh(mesh.devices.reshape(4, 2, mesh.shape["col"]), ("row_0", "row_1", "col"))
    in_specs = (
        P(ROW_COL, None),
        P(),
        P(),
        P(ROW_COL, None),
        P(ROW_COL, None, None),
        P(ROW_COL, None),
    )
    out_specs = (P(ROW_COL, None), P(ROW_COL, None), P(ROW_COL, None), P(ROW_COL))
    return jax.shard_map(local, mesh=split, in_specs=in_specs, out_specs=out_specs, check_vma=False)
```

profile of v0, /device:TPU:8, one launch (start us, length us, event | category | flops | bytes accessed | tf_op | source)
XLA Modules:
  0.0 879.9 jit_solution(5137925944958161656)
XLA Ops:
  7.2 0.0 all-gather.7.cloned.1.call-start
  7.2 20.7 %all-gather = bf16[1024,256]{1,0:T(8,128)(2,1)} all-gather(bf16[256,256]{1,0:T(8,128)(2,1)} %param.10), channel_id=2, replica_groups=mesh['row_0'=4,'row_1'=2,'col'=32] {'row_0'}, dimensions={0}, use_global_device_ids=true | all-gather | bytes 655360 | tf_op jit(solution)/shard_map/all_gather | solution.py:21
  27.9 0.0 all-gather.9.cloned.1.call-start
  28.0 0.7 all-gather.9.cloned.1.call-update
  28.7 0.8 compare_and_fusion
  29.5 0.7 bitcast_convert_fusion
  30.2 0.8 fusion.27
  30.9 11.1 %all-gather.7.cloned.1.call-done = bf16[8,256,256]{2,1,0:T(8,128)(2,1)} async-done(((bf16[4,256,256]{2,1,0:T(8,128)(2,1)}), bf16[8,256,256]{2,1,0:T(8,128)(2,1)}) %all-gather.7.cloned.1.call-update) | async-done | bytes 1048592 | tf_op jit(solution)/shard_map/all_gather | solution.py:21
  42.0 1.3 copy.37
  43.3 2.8 gather_fusion
  46.1 8.7 multiply_bitcast_fusion.3
  54.8 9.0 %copy.39 = f32[32,256,256]{2,1,0:T(8,128)} copy(f32[32,256,256]{1,2,0:T(8,128)} %multiply_bitcast_fusion.3) | data formatting | bytes 16777216 | tf_op jit(solution)/shard_map/mul | solution.py:89
  63.8 4.2 broadcast.111.clone
  67.9 18.3 %scatter_fusion = f32[32,256,256]{2,1,0:T(8,128)} fusion(f32[32,256,256]{2,1,0:T(8,128)} %broadcast.111.clone, s32[32]{0:T(128)S(1)} %get-tuple-element.16, f32[32,256,256]{2,1,0:T(8,128)} %copy.39), kind=kCustom, calls=%fused_computation.4 | custom fusion | flops 2097152 | bytes 25165952 | tf_op jit(solution)/shard_map/scatter-add | solution.py:89
  86.2 5.9 convert_element_type.70
  92.2 8.4 all-to-all-start
  100.6 0.0 reduce-scatter.5.cloned.1.call-start
  100.6 122.7 %all-gather.9.cloned.1.call-done = bf16[8192,256]{1,0:T(8,128)(2,1)} async-done(((bf16[256,256]{1,0:T(8,128)(2,1)}), bf16[8192,256]{1,0:T(8,128)(2,1)}) %all-gather.9.cloned.1.call-update) | async-done | bytes 4194320 | tf_op jit(solution)/shard_map/all_gather | solution.py:65
  223.4 5.0 gather_fusion.1
  228.3 8.6 multiply_bitcast_fusion.2
  236.9 9.0 %copy.41 = f32[32,256,256]{2,1,0:T(8,128)} copy(f32[32,256,256]{1,2,0:T(8,128)} %multiply_bitcast_fusion.2) | data formatting | bytes 16777216 | tf_op jit(solution)/shard_map/mul | solution.py:94
  245.9 0.2 broadcast.114.clone
  246.1 11.6 %scatter_fusion.1 = f32[8,256,256]{2,1,0:T(8,128)S(1)} fusion(f32[8,256,256]{2,1,0:T(8,128)S(1)} %broadcast.114.clone, s32[32]{0:T(128)S(1)} %get-tuple-element.15, f32[32,256,256]{2,1,0:T(8,128)} %copy.41), kind=kCustom, calls=%fused_computation.5 | custom fusion | flops 2097152 | bytes 25165952 | tf_op jit(solution)/shard_map/scatter-add | solution.py:94
  257.7 0.1 convert_element_type.72
  257.8 1.1 copy.42
  258.9 0.0 reduce-scatter.7.cloned.1.call-start
  259.0 23.5 %reduce-scatter.5.cloned.1.call-done = bf16[4,256,256]{2,1,0:T(8,128)(2,1)} async-done(((bf16[8,256,256]{2,1,0:T(8,128)(2,1)}), bf16[4,256,256]{2,1,0:T(8,128)(2,1)}) %reduce-scatter.5.cloned.1.call-update) | async-done | bytes 524304 | tf_op jit(solution)/shard_map/reduce_scatter | solution.py:50
  282.5 0.0 all-gather.11.cloned.1.call-start
  282.5 2.8 convert_reduce_fusion.1
  285.3 28.8 %reduce-scatter.7.cloned.1.call-done = bf16[1,256,256]{2,1,0:T(8,128)(2,1)} async-done(((bf16[4,256,256]{2,1,0:T(8,128)(2,1)}), bf16[1,256,256]{2,1,0:T(8,128)(2,1)}) %reduce-scatter.7.cloned.1.call-update) | async-done | bytes 131088 | tf_op jit(solution)/shard_map/reduce_scatter | solution.py:50
  314.2 1.9 convert_reduce_fusion.2
  316.0 0.2 convolution_convert_fusion
  316.3 17.2 %all-gather.1 = bf16[1024,256]{1,0:T(8,128)(2,1)} all-gather(bf16[256,256]{1,0:T(8,128)(2,1)S(1)} %convolution_convert_fusion), channel_id=3, replica_groups=mesh['row_0'=4,'row_1'=2,'col'=32] {'row_0'}, dimensions={0}, use_global_device_ids=true | all-gather | bytes 655360 | tf_op jit(solution)/shard_map/all_gather | solution.py:21
  333.5 0.2 all-gather.13.cloned.1.call-start
  333.7 0.3 all-gather.13.cloned.1.call-update
  334.0 12.4 %all-gather.11.cloned.1.call-done = bf16[8,256,256]{2,1,0:T(8,128)(2,1)} async-done(((bf16[4,256,256]{2,1,0:T(8,128)(2,1)}), bf16[8,256,256]{2,1,0:T(8,128)(2,1)}) %all-gather.11.cloned.1.call-update) | async-done | bytes 1048592 | tf_op jit(solution)/shard_map/all_gather | solution.py:21
  346.5 1.3 copy.43
  347.8 2.8 gather_fusion.2
  350.5 8.6 multiply_bitcast_fusion.1
  359.1 9.0 %copy.45 = f32[32,256,256]{2,1,0:T(8,128)} copy(f32[32,256,256]{1,2,0:T(8,128)} %multiply_bitcast_fusion.1) | data formatting | bytes 16777216 | tf_op jit(solution)/shard_map/mul | solution.py:89
  368.1 4.2 broadcast.111
  372.3 18.9 %scatter_fusion.2 = f32[32,256,256]{2,1,0:T(8,128)} fusion(f32[32,256,256]{2,1,0:T(8,128)} %broadcast.111, s32[32]{0:T(128)S(1)} %get-tuple-element.16, f32[32,256,256]{2,1,0:T(8,128)} %copy.45), kind=kCustom, calls=%fused_computation.6 | custom fusion | flops 2097152 | bytes 25165952 | tf_op jit(solution)/shard_map/scatter-add | solution.py:89
  391.2 5.9 convert_element_type.81
  397.1 8.4 all-to-all-start.1
  405.6 0.0 reduce-scatter.9.cloned.1.call-start
  405.6 121.7 %all-gather.13.cloned.1.call-done = bf16[8192,256]{1,0:T(8,128)(2,1)} async-done(((bf16[256,256]{1,0:T(8,128)(2,1)}), bf16[8192,256]{1,0:T(8,128)(2,1)}) %all-gather.13.cloned.1.call-update) | async-done | bytes 4194320 | tf_op jit(solution)/shard_map/all_gather | solution.py:65
  527.3 4.9 gather_fusion.3
  532.2 8.6 multiply_bitcast_fusion
  540.9 9.0 %copy.47 = f32[32,256,256]{2,1,0:T(8,128)} copy(f32[32,256,256]{1,2,0:T(8,128)} %multiply_bitcast_fusion) | data formatting | bytes 16777216 | tf_op jit(solution)/shard_map/mul | solution.py:94
  549.8 0.2 broadcast.114
  550.0 11.6 %scatter_fusion.3 = f32[8,256,256]{2,1,0:T(8,128)S(1)} fusion(f32[8,256,256]{2,1,0:T(8,128)S(1)} %broadcast.114, s32[32]{0:T(128)S(1)} %get-tuple-element.15, f32[32,256,256]{2,1,0:T(8,128)} %copy.47), kind=kCustom, calls=%fused_computation.7 | custom fusion | flops 2097152 | bytes 25165952 | tf_op jit(solution)/shard_map/scatter-add | solution.py:94
  561.7 0.1 convert_element_type.83
  561.8 1.0 copy.48
  562.9 0.0 all-reduce.4.cloned.1.call-start
  562.9 0.9 convolution_multiply_fusion
  563.9 0.0 reduce-scatter.11.cloned.1.call-start
  563.9 21.4 %reduce-scatter.9.cloned.1.call-done = bf16[4,256,256]{2,1,0:T(8,128)(2,1)} async-done(((bf16[8,256,256]{2,1,0:T(8,128)(2,1)}), bf16[4,256,256]{2,1,0:T(8,128)(2,1)}) %reduce-scatter.9.cloned.1.call-update) | async-done | bytes 524304 | tf_op jit(solution)/shard_map/reduce_scatter | solution.py:50
  585.4 76.3 %all-reduce.1 = f32[256]{0:T(256)S(1)} all-reduce(f32[256]{0:T(256)S(1)} %broadcast_multiply_fusion), channel_id=9, replica_groups=mesh['row_0'=4,'row_1'=2,'col'=32] {'row_0','row_1','col'}, use_global_device_ids=true, to_apply=%region_12.15.clone | all-reduce | flops 256 | bytes 2048
  661.7 0.6 dynamic-slice.1
  662.3 180.3 %all-reduce.4.cloned.1.call-done = f32[256,256]{1,0:T(8,128)} async-done(((f32[256,256]{1,0:T(8,128)}), f32[256,256]{1,0:T(8,128)}) %all-reduce.4.cloned.1.call-update) | async-done | bytes 262160
  842.6 1.3 constant_dynamic-slice_fusion
  843.8 2.8 convert_reduce_fusion
  846.6 25.2 %reduce-scatter.11.cloned.1.call-done = bf16[1,256,256]{2,1,0:T(8,128)(2,1)} async-done(((bf16[4,256,256]{2,1,0:T(8,128)(2,1)}), bf16[1,256,256]{2,1,0:T(8,128)(2,1)}) %reduce-scatter.11.cloned.1.call-update) | async-done | bytes 131088 | tf_op jit(solution)/shard_map/reduce_scatter | solution.py:50
  871.8 1.6 fusion.24
  (24 shorter events, 0.2 us)
Async XLA Ops:
  7.2 307.0 %copy-start = (bf16[256,256]{1,0:T(8,128)(2,1)S(1)}, bf16[256,256]{1,0:T(8,128)(2,1)}, u32[]{:S(2)}) copy-start(bf16[256,256]{1,0:T(8,128)(2,1)} %param.11) | copy-start | bytes 393220
  7.2 34.9 %all-gather.7.cloned.1.call-start = ((), (), s32[]{:S(2)}) async-start(), calls=%async_computation.6 | async-start | bytes 1572864 | tf_op jit(solution)/shard_map/all_gather | solution.py:21
  27.9 195.4 %all-gather.9.cloned.1.call-start = ((), (), s32[]{:S(2)}) async-start(), calls=%async_computation.7 | async-start | bytes 4325376 | tf_op jit(solution)/shard_map/all_gather | solution.py:65
  92.2 190.4 %all-to-all-start = ((bf16[32,256,256]{2,1,0:T(8,128)(2,1)}), bf16[32,256,256]{2,1,0:T(8,128)(2,1)}, u32[]{:S(2)}, u32[]{:S(2)}) async-start(bf16[32,256,256]{2,1,0:T(8,128)(2,1)} %convert_element_type.70), calls=%async_computation | async-start | bytes 8388608 | tf_op jit(solution)/shard_map/all_to_all | solution.py:40
  100.6 181.9 %reduce-scatter.5.cloned.1.call-start = ((), (), s32[]{:S(2)}) async-start(), calls=%async_computation.8 | async-start | bytes 1572864 | tf_op jit(solution)/shard_map/reduce_scatter | solution.py:50
  257.8 56.4 %copy-start.4 = (bf16[256,256]{1,0:T(8,128)(2,1)S(1)}, bf16[256,256]{1,0:T(8,128)(2,1)}, u32[]{:S(2)}) copy-start(bf16[256,256]{1,0:T(8,128)(2,1)} %param.13) | copy-start | bytes 393220
  257.8 56.4 %copy-start.5 = (f32[256]{0:T(256)S(1)}, f32[256]{0:T(256)}, u32[]{:S(2)}) copy-start(f32[256]{0:T(256)} %param.12) | copy-start | bytes 3076
  258.9 55.3 %reduce-scatter.7.cloned.1.call-start = ((), (), s32[]{:S(2)}) async-start(), calls=%async_computation.9 | async-start | bytes 655360 | tf_op jit(solution)/shard_map/reduce_scatter | solution.py:50
  282.5 64.0 %all-gather.11.cloned.1.call-start = ((), (), s32[]{:S(2)}) async-start(), calls=%async_computation.10 | async-start | bytes 1572864 | tf_op jit(solution)/shard_map/all_gather | solution.py:21
  316.3 17.4 %copy-start.2 = (bf16[256,256]{1,0:T(8,128)(2,1)}, bf16[256,256]{1,0:T(8,128)(2,1)S(1)}, u32[]{:S(2)}) copy-start(bf16[256,256]{1,0:T(8,128)(2,1)S(1)} %convolution_convert_fusion) | copy-start | bytes 393220
  333.5 193.8 %all-gather.13.cloned.1.call-start = ((), (), s32[]{:S(2)}) async-start(), calls=%async_computation.11 | async-start | bytes 4325376 | tf_op jit(solution)/shard_map/all_gather | solution.py:65
  397.1 446.7 %all-to-all-start.1 = ((bf16[32,256,256]{2,1,0:T(8,128)(2,1)}), bf16[32,256,256]{2,1,0:T(8,128)(2,1)}, u32[]{:S(2)}, u32[]{:S(2)}) async-start(bf16[32,256,256]{2,1,0:T(8,128)(2,1)} %convert_element_type.81), calls=%async_computation.3 | async-start | bytes 8388608 | tf_op jit(solution)/shard_map/all_to_all | solution.py:40
  405.6 179.8 %reduce-scatter.9.cloned.1.call-start = ((), (), s32[]{:S(2)}) async-start(), calls=%async_computation.12 | async-start | bytes 1572864 | tf_op jit(solution)/shard_map/reduce_scatter | solution.py:50
  561.6 1.3 copy-start.3
  561.8 311.6 %copy-start.1 = (bf16[256,256]{1,0:T(8,128)(2,1)S(1)}, bf16[256,256]{1,0:T(8,128)(2,1)}, u32[]{:S(2)}) copy-start(bf16[256,256]{1,0:T(8,128)(2,1)} %param.11) | copy-start | bytes 393220
  562.9 279.7 %all-reduce.4.cloned.1.call-start = ((), (), s32[]{:S(2)}) async-start(), calls=%async_computation.14 | async-start | bytes 524288
  563.9 307.9 %reduce-scatter.11.cloned.1.call-start = ((), (), s32[]{:S(2)}) async-start(), calls=%async_computation.13 | async-start | bytes 655360 | tf_op jit(solution)/shard_map/reduce_scatter | solution.py:50
Sparse Core Ops, SparseCore 0:
  28.1 13.9 all-gather.6
  43.8 179.4 all-gather.8
  259.0 23.3 reduce-scatter.4
  285.0 29.1 reduce-scatter.6
  333.6 12.8 all-gather.10
  348.8 178.3 all-gather.12
  563.0 22.3 reduce-scatter.8
  590.8 251.6 all-reduce.3
  845.1 26.6 reduce-scatter.10
where the time goes:
time: 882 us; the launch traced here: 880 us
  waiting for transfers between devices  548 us (62%)
  blocking collectives  114 us (13%)
  other arithmetic  81.9 us (9%)
  local copies, waits for them, and re-layouts  66.6 us (8%)
  matrix products  37.6 us (4%)
  starting transfers between devices  17.4 us (2%)
  between operations  14 us (2%)
    all_gather x2, waiting for transfers between devices, aggregate(): row_group = lax.all_gather(node_data, 'col', axis=0, tiled=True)  244 us
    unnamed x10, waiting for transfers between devices  181 us
    reduce_scatter x4, waiting for transfers between devices, sum_in_order(): blocks = lax.psum_scatter(blocks, axes[k], scatter_dimension=0, tiled=True)  99 us
    unnamed x1, blocking collectives  76.3 us
    all_gather x2, blocking collectives, stacked_from(): blocks = lax.all_gather(blocks, axes[k], axis=0, tiled=True)  37.8 us
    scatter-add x2, other arithmetic, aggregate(): row_partial = jnp.zeros((row_span, tile_size, feature_count), jnp.float32...  37.2 us
    all_gather x2, waiting for transfers between devices, stacked_from(): blocks = lax.all_gather(blocks, axes[k], axis=0, tiled=True)  23.5 us
    scatter-add x2, other arithmetic, aggregate(): column_partial = jnp.zeros((column_span, tile_size, feature_count), jnp.f...  23.3 us
  transfers between devices with their start and end apart: 11, of which 9 were waited for; matrix products, arithmetic and copies ran while one was open for 21% of the time, Pallas kernels for 0%

commit v1 on v0

--- a/solution.py
+++ b/solution.py
@@ -62,7 +62,9 @@
     column_devices = lax.axis_size("col")
     row_index = lax.axis_index(ROW)
     column_group = gathered_by_axis(node_data, ROW, (0, 1), 0)
-    row_group = lax.all_gather(node_data, "col", axis=0, tiled=True)
+    row_group = jnp.concatenate(
+        lax.all_to_all(jnp.stack([node_data] * lax.axis_size("col")), "col", 0, 0), axis=0
+    )
     column_blocks = column_group.reshape(-1, tile_size, feature_count)
     row_blocks = row_group.reshape(-1, tile_size, feature_count)
     row_span = row_blocks.shape[0]

time: 882 us -> 743 us (0.84)
  waiting for transfers between devices: 548 us -> 282 us
  blocking collectives: 114 us -> 222 us
  starting transfers between devices: 17.4 us -> 34.2 us
    all_gather x2 -> x0, waiting for transfers between devices: 244 us -> none  [aggregate(): row_group = lax.all_gather(node_data, 'col', axis=0, tiled=True)]
    all_gather x2, blocking collectives: 37.8 us -> 143 us  [stacked_from(): blocks = lax.all_gather(blocks, axes[k], axis=0, tiled=True)]
    reduce_scatter x4, waiting for transfers between devices: 99 us -> 71.6 us  [sum_in_order(): blocks = lax.psum_scatter(blocks, axes[k], scatter_dimension=0, tiled=True)]
    all_to_all x0 -> x2, starting transfers between devices: none -> 17.3 us  [aggregate(): lax.all_to_all(jnp.stack([node_data] * lax.axis_size('col')), 'col', 0, 0)]
    all_to_all x2, waiting for transfers between devices: 0.01 us -> 10.2 us  [sent_and_summed(): lax.all_to_all(split_up(array, dim, length), axis, 0, 0, tiled=True)]
    unnamed x10 -> x8, waiting for transfers between devices: 181 us -> 178 us
  transfers between devices with their start and end apart: 11 -> 11, of which waited for: 9 -> 8; matrix products, arithmetic and copies ran while one was open for 21% -> 24% of each run, Pallas kernels for 0% -> 0%
where the time goes in v1:
time: 743 us; the launch traced here: 742 us
  waiting for transfers between devices  282 us (38%)
  blocking collectives  222 us (30%)
  other arithmetic  79.2 us (11%)
  local copies, waits for them, and re-layouts  72.4 us (10%)
  matrix products  37.5 us (5%)
  starting transfers between devices  34.2 us (5%)
  between operations  14.4 us (2%)
    unnamed x8, waiting for transfers between devices  178 us
    all_gather x2, blocking collectives, stacked_from(): blocks = lax.all_gather(blocks, axes[k], axis=0, tiled=True)  143 us
    unnamed x1, blocking collectives  78.8 us
    reduce_scatter x4, waiting for transfers between devices, sum_in_order(): blocks = lax.psum_scatter(blocks, axes[k], scatter_dimension=0, tiled=True)  71.6 us
    scatter-add x2, other arithmetic, aggregate(): row_partial = jnp.zeros((row_span, tile_size, feature_count), jnp.float32...  36.6 us
    scatter-add x2, other arithmetic, aggregate(): column_partial = jnp.zeros((column_span, tile_size, feature_count), jnp.f...  23.3 us
    all_gather x2, waiting for transfers between devices, stacked_from(): blocks = lax.all_gather(blocks, axes[k], axis=0, tiled=True)  22.1 us
    mul x2, local copies, waits for them, and re-layouts, aggregate(): mirror_terms * live  17.9 us
  transfers between devices with their start and end apart: 11, of which 8 were waited for; matrix products, arithmetic and copies ran while one was open for 24% of the time, Pallas kernels for 0%

profile of v1, /device:TPU:8, one launch (start us, length us, event | category | flops | bytes accessed | tf_op | source)
XLA Modules:
  0.0 741.6 jit_solution(11563763875444608248)
XLA Ops:
  7.2 3.4 stack.4
  10.6 9.1 %all-to-all-start.1 = ((bf16[32,256,256]{2,1,0:T(8,128)(2,1)}), bf16[32,256,256]{2,1,0:T(8,128)(2,1)}, u32[]{:S(2)}, u32[]{:S(2)}) async-start(bf16[32,256,256]{2,1,0:T(8,128)(2,1)} %stack.4), calls=%async_computation.1 | async-start | bytes 8388608 | tf_op jit(solution)/shard_map/all_to_all | solution.py:66
  19.6 0.0 all-gather.5.cloned.1.call-start
  19.7 77.1 %all-gather = bf16[1024,256]{1,0:T(8,128)(2,1)} all-gather(bf16[256,256]{1,0:T(8,128)(2,1)S(1)} %copy-done.2), channel_id=2, replica_groups=mesh['row_0'=4,'row_1'=2,'col'=32] {'row_0'}, dimensions={0}, use_global_device_ids=true | all-gather | bytes 655360 | tf_op jit(solution)/shard_map/all_gather | solution.py:21
  96.8 0.0 all-gather.5.cloned.1.call-update
  96.9 9.4 %all-gather.5.cloned.1.call-done = bf16[8,256,256]{2,1,0:T(8,128)(2,1)} async-done(((bf16[4,256,256]{2,1,0:T(8,128)(2,1)}), bf16[8,256,256]{2,1,0:T(8,128)(2,1)}) %all-gather.5.cloned.1.call-update) | async-done | bytes 1048592 | tf_op jit(solution)/shard_map/all_gather | solution.py:21
  106.3 1.3 copy.37
  107.6 2.8 gather_fusion
  110.4 8.6 %multiply_bitcast_fusion.3 = f32[32,256,256]{1,2,0:T(8,128)} fusion(f32[32]{0:T(128)S(1)} %bitcast_convert_fusion, bf16[32,256,256]{2,1,0:T(8,128)(2,1)} %param.14, bf16[32,256,256]{2,1,0:T(8,128)(2,1)} %gather_fusion, pred[32]{0:T(512)(128)(4,1)S(1)} %get-tuple-element.13), kind=kOutput, calls=%fused_computation.13 | convolution fusion | flops 1077936128 | bytes 16777376 | tf_op jit(solution)/shard_map/tnm,tmf->tnf/dot_general | solution.py:81
  119.0 9.0 %copy.39 = f32[32,256,256]{2,1,0:T(8,128)} copy(f32[32,256,256]{1,2,0:T(8,128)} %multiply_bitcast_fusion.3) | data formatting | bytes 16777216 | tf_op jit(solution)/shard_map/mul | solution.py:91
  128.0 4.2 broadcast.115.clone
  132.2 18.3 %scatter_fusion = f32[32,256,256]{2,1,0:T(8,128)} fusion(f32[32,256,256]{2,1,0:T(8,128)} %broadcast.115.clone, s32[32]{0:T(128)S(1)} %get-tuple-element.16, f32[32,256,256]{2,1,0:T(8,128)} %copy.39), kind=kCustom, calls=%fused_computation.4 | custom fusion | flops 2097152 | bytes 25165952 | tf_op jit(solution)/shard_map/scatter-add | solution.py:91
  150.5 5.9 convert_element_type.70
  156.4 8.3 %all-to-all-start = ((bf16[32,256,256]{2,1,0:T(8,128)(2,1)}), bf16[32,256,256]{2,1,0:T(8,128)(2,1)}, u32[]{:S(2)}, u32[]{:S(2)}) async-start(bf16[32,256,256]{2,1,0:T(8,128)(2,1)} %convert_element_type.70), calls=%async_computation | async-start | bytes 8388608 | tf_op jit(solution)/shard_map/all_to_all | solution.py:40
  164.7 0.0 reduce-scatter.5.cloned.1.call-start
  164.8 5.0 gather_fusion.1
  169.8 8.6 %multiply_bitcast_fusion.2 = f32[32,256,256]{1,2,0:T(8,128)} fusion(f32[32]{0:T(128)S(1)} %bitcast_convert_fusion, bf16[32,256,256]{2,1,0:T(8,128)(2,1)} %param.14, bf16[32,256,256]{2,1,0:T(8,128)(2,1)} %gather_fusion.1, pred[32]{0:T(512)(128)(4,1)S(1)} %get-tuple-element.8), kind=kOutput, calls=%fused_computation.11 | convolution fusion | flops 1077936128 | bytes 16777376 | tf_op jit(solution)/shard_map/tmn,tmf->tnf/dot_general | solution.py:84
  178.4 9.0 %copy.41 = f32[32,256,256]{2,1,0:T(8,128)} copy(f32[32,256,256]{1,2,0:T(8,128)} %multiply_bitcast_fusion.2) | data formatting | bytes 16777216 | tf_op jit(solution)/shard_map/mul | solution.py:96
  187.3 0.2 broadcast.118.clone
  187.5 11.6 %scatter_fusion.1 = f32[8,256,256]{2,1,0:T(8,128)S(1)} fusion(f32[8,256,256]{2,1,0:T(8,128)S(1)} %broadcast.118.clone, s32[32]{0:T(128)S(1)} %get-tuple-element.15, f32[32,256,256]{2,1,0:T(8,128)} %copy.41), kind=kCustom, calls=%fused_computation.5 | custom fusion | flops 2097152 | bytes 25165952 | tf_op jit(solution)/shard_map/scatter-add | solution.py:96
  199.2 0.1 convert_element_type.72
  199.3 1.1 copy.42
  200.4 0.0 reduce-scatter.5.cloned.1.call-update
  200.4 0.0 reduce-scatter.7.cloned.1.call-start
  200.4 14.7 %reduce-scatter.5.cloned.1.call-done = bf16[4,256,256]{2,1,0:T(8,128)(2,1)} async-done(((bf16[8,256,256]{2,1,0:T(8,128)(2,1)}), bf16[4,256,256]{2,1,0:T(8,128)(2,1)}) %reduce-scatter.5.cloned.1.call-update) | async-done | bytes 524304 | tf_op jit(solution)/shard_map/reduce_scatter | solution.py:50
  215.1 0.0 reduce-scatter.7.cloned.1.call-update
  215.1 10.2 %all-to-all-done = bf16[32,256,256]{2,1,0:T(8,128)(2,1)} async-done(((bf16[32,256,256]{2,1,0:T(8,128)(2,1)}), bf16[32,256,256]{2,1,0:T(8,128)(2,1)}, u32[]{:S(2)}, u32[]{:S(2)}) %all-to-all-start) | async-done | bytes 4194336 | tf_op jit(solution)/shard_map/all_to_all | solution.py:40
  225.4 2.8 convert_reduce_fusion.1
  228.2 18.1 %reduce-scatter.7.cloned.1.call-done = bf16[1,256,256]{2,1,0:T(8,128)(2,1)} async-done(((bf16[4,256,256]{2,1,0:T(8,128)(2,1)}), bf16[1,256,256]{2,1,0:T(8,128)(2,1)}) %reduce-scatter.7.cloned.1.call-update) | async-done | bytes 131088 | tf_op jit(solution)/shard_map/reduce_scatter | solution.py:50
  246.3 1.9 convert_reduce_fusion.2
  248.1 0.2 convolution_convert_fusion
  248.3 2.4 stack.5
  250.8 8.2 %all-to-all-start.3 = ((bf16[32,256,256]{2,1,0:T(8,128)(2,1)}), bf16[32,256,256]{2,1,0:T(8,128)(2,1)}, u32[]{:S(2)}, u32[]{:S(2)}) async-start(bf16[32,256,256]{2,1,0:T(8,128)(2,1)} %stack.5), calls=%async_computation.5 | async-start | bytes 8388608 | tf_op jit(solution)/shard_map/all_to_all | solution.py:66
  259.0 0.0 all-gather.7.cloned.1.call-start
  259.0 66.0 %all-gather.1 = bf16[1024,256]{1,0:T(8,128)(2,1)} all-gather(bf16[256,256]{1,0:T(8,128)(2,1)S(1)} %convolution_convert_fusion), channel_id=3, replica_groups=mesh['row_0'=4,'row_1'=2,'col'=32] {'row_0'}, dimensions={0}, use_global_device_ids=true | all-gather | bytes 655360 | tf_op jit(solution)/shard_map/all_gather | solution.py:21
  325.1 0.0 all-gather.7.cloned.1.call-update
  325.1 12.7 %all-gather.7.cloned.1.call-done = bf16[8,256,256]{2,1,0:T(8,128)(2,1)} async-done(((bf16[4,256,256]{2,1,0:T(8,128)(2,1)}), bf16[8,256,256]{2,1,0:T(8,128)(2,1)}) %all-gather.7.cloned.1.call-update) | async-done | bytes 1048592 | tf_op jit(solution)/shard_map/all_gather | solution.py:21
  337.8 1.3 copy.43
  339.1 2.8 gather_fusion.2
  341.9 8.6 %multiply_bitcast_fusion.1 = f32[32,256,256]{1,2,0:T(8,128)} fusion(f32[32]{0:T(128)S(1)} %bitcast_convert_fusion, bf16[32,256,256]{2,1,0:T(8,128)(2,1)} %param.14, bf16[32,256,256]{2,1,0:T(8,128)(2,1)} %gather_fusion.2, pred[32]{0:T(512)(128)(4,1)S(1)} %get-tuple-element.13), kind=kOutput, calls=%fused_computation.10 | convolution fusion | flops 1077936128 | bytes 16777376 | tf_op jit(solution)/shard_map/tnm,tmf->tnf/dot_general | solution.py:81
  350.5 9.0 %copy.45 = f32[32,256,256]{2,1,0:T(8,128)} copy(f32[32,256,256]{1,2,0:T(8,128)} %multiply_bitcast_fusion.1) | data formatting | bytes 16777216 | tf_op jit(solution)/shard_map/mul | solution.py:91
  359.4 4.2 broadcast.115
  363.6 18.3 %scatter_fusion.2 = f32[32,256,256]{2,1,0:T(8,128)} fusion(f32[32,256,256]{2,1,0:T(8,128)} %broadcast.115, s32[32]{0:T(128)S(1)} %get-tuple-element.16, f32[32,256,256]{2,1,0:T(8,128)} %copy.45), kind=kCustom, calls=%fused_computation.6 | custom fusion | flops 2097152 | bytes 25165952 | tf_op jit(solution)/shard_map/scatter-add | solution.py:91
  381.9 5.9 convert_element_type.81
  387.8 8.3 %all-to-all-start.2 = ((bf16[32,256,256]{2,1,0:T(8,128)(2,1)}), bf16[32,256,256]{2,1,0:T(8,128)(2,1)}, u32[]{:S(2)}, u32[]{:S(2)}) async-start(bf16[32,256,256]{2,1,0:T(8,128)(2,1)} %convert_element_type.81), calls=%async_computation.4 | async-start | bytes 8388608 | tf_op jit(solution)/shard_map/all_to_all | solution.py:40
  396.1 0.0 reduce-scatter.9.cloned.1.call-start
  396.2 5.0 gather_fusion.3
  401.2 8.6 %multiply_bitcast_fusion = f32[32,256,256]{1,2,0:T(8,128)} fusion(f32[32]{0:T(128)S(1)} %bitcast_convert_fusion, bf16[32,256,256]{2,1,0:T(8,128)(2,1)} %param.14, bf16[32,256,256]{2,1,0:T(8,128)(2,1)} %gather_fusion.3, pred[32]{0:T(512)(128)(4,1)S(1)} %get-tuple-element.8), kind=kOutput, calls=%fused_computation.8 | convolution fusion | flops 1077936128 | bytes 16777376 | tf_op jit(solution)/shard_map/tmn,tmf->tnf/dot_general | solution.py:84
  409.8 9.0 %copy.47 = f32[32,256,256]{2,1,0:T(8,128)} copy(f32[32,256,256]{1,2,0:T(8,128)} %multiply_bitcast_fusion) | data formatting | bytes 16777216 | tf_op jit(solution)/shard_map/mul | solution.py:96
  418.8 0.2 broadcast.118
  418.9 11.6 %scatter_fusion.3 = f32[8,256,256]{2,1,0:T(8,128)S(1)} fusion(f32[8,256,256]{2,1,0:T(8,128)S(1)} %broadcast.118, s32[32]{0:T(128)S(1)} %get-tuple-element.15, f32[32,256,256]{2,1,0:T(8,128)} %copy.47), kind=kCustom, calls=%fused_computation.7 | custom fusion | flops 2097152 | bytes 25165952 | tf_op jit(solution)/shard_map/scatter-add | solution.py:96
  430.6 0.1 convert_element_type.83
  430.7 1.0 copy.48
  431.8 0.0 all-reduce.4.cloned.1.call-start
  431.8 0.9 convolution_multiply_fusion
  432.8 0.0 reduce-scatter.11.cloned.1.call-start
  432.9 13.6 %reduce-scatter.9.cloned.1.call-done = bf16[4,256,256]{2,1,0:T(8,128)(2,1)} async-done(((bf16[8,256,256]{2,1,0:T(8,128)(2,1)}), bf16[4,256,256]{2,1,0:T(8,128)(2,1)}) %reduce-scatter.9.cloned.1.call-update) | async-done | bytes 524304 | tf_op jit(solution)/shard_map/reduce_scatter | solution.py:50
  446.6 78.8 %all-reduce.1 = f32[256]{0:T(256)S(1)} all-reduce(f32[256]{0:T(256)S(1)} %broadcast_multiply_fusion), channel_id=9, replica_groups=mesh['row_0'=4,'row_1'=2,'col'=32] {'row_0','row_1','col'}, use_global_device_ids=true, to_apply=%region_12.15.clone | all-reduce | flops 256 | bytes 2048
  525.4 0.6 dynamic-slice.1
  526.0 178.0 %all-reduce.4.cloned.1.call-done = f32[256,256]{1,0:T(8,128)} async-done(((f32[256,256]{1,0:T(8,128)}), f32[256,256]{1,0:T(8,128)}) %all-reduce.4.cloned.1.call-update) | async-done | bytes 262160
  703.9 1.3 constant_dynamic-slice_fusion
  705.2 2.8 convert_reduce_fusion
  708.0 25.2 %reduce-scatter.11.cloned.1.call-done = bf16[1,256,256]{2,1,0:T(8,128)(2,1)} async-done(((bf16[4,256,256]{2,1,0:T(8,128)(2,1)}), bf16[1,256,256]{2,1,0:T(8,128)(2,1)}) %reduce-scatter.11.cloned.1.call-update) | async-done | bytes 131088 | tf_op jit(solution)/shard_map/reduce_scatter | solution.py:50
  733.2 1.6 fusion.24
  (26 shorter events, 0.2 us)
Async XLA Ops:
  7.2 239.1 %copy-start = (bf16[256,256]{1,0:T(8,128)(2,1)S(1)}, bf16[256,256]{1,0:T(8,128)(2,1)}, u32[]{:S(2)}) copy-start(bf16[256,256]{1,0:T(8,128)(2,1)} %param.11) | copy-start | bytes 393220
  10.6 9.1 %copy-start.2 = (bf16[256,256]{1,0:T(8,128)(2,1)S(1)}, bf16[256,256]{1,0:T(8,128)(2,1)}, u32[]{:S(2)}) copy-start(bf16[256,256]{1,0:T(8,128)(2,1)} %param.10) | copy-start | bytes 393220
  10.6 86.3 %copy-start.4 = (s32[32,2]{0,1:T(2,128)S(1)}, s32[32,2]{0,1:T(2,128)}, u32[]{:S(2)}) copy-start(s32[32,2]{0,1:T(2,128)} %param.15) | copy-start | bytes 772
  10.6 145.8 %all-to-all-start.1 = ((bf16[32,256,256]{2,1,0:T(8,128)(2,1)}), bf16[32,256,256]{2,1,0:T(8,128)(2,1)}, u32[]{:S(2)}, u32[]{:S(2)}) async-start(bf16[32,256,256]{2,1,0:T(8,128)(2,1)} %stack.4), calls=%async_computation.1 | async-start | bytes 8388608 | tf_op jit(solution)/shard_map/all_to_all | solution.py:66
  19.6 86.7 %all-gather.5.cloned.1.call-start = ((), (), s32[]{:S(2)}) async-start(), calls=%async_computation.8 | async-start | bytes 1572864 | tf_op jit(solution)/shard_map/all_gather | solution.py:21
  156.4 69.0 %all-to-all-start = ((bf16[32,256,256]{2,1,0:T(8,128)(2,1)}), bf16[32,256,256]{2,1,0:T(8,128)(2,1)}, u32[]{:S(2)}, u32[]{:S(2)}) async-start(bf16[32,256,256]{2,1,0:T(8,128)(2,1)} %convert_element_type.70), calls=%async_computation | async-start | bytes 8388608 | tf_op jit(solution)/shard_map/all_to_all | solution.py:40
  164.7 50.4 %reduce-scatter.5.cloned.1.call-start = ((), (), s32[]{:S(2)}) async-start(), calls=%async_computation.9 | async-start | bytes 1572864 | tf_op jit(solution)/shard_map/reduce_scatter | solution.py:50
  199.3 47.0 %copy-start.5 = (bf16[256,256]{1,0:T(8,128)(2,1)S(1)}, bf16[256,256]{1,0:T(8,128)(2,1)}, u32[]{:S(2)}) copy-start(bf16[256,256]{1,0:T(8,128)(2,1)} %param.13) | copy-start | bytes 393220
  199.3 47.0 %copy-start.6 = (f32[256]{0:T(256)S(1)}, f32[256]{0:T(256)}, u32[]{:S(2)}) copy-start(f32[256]{0:T(256)} %param.12) | copy-start | bytes 3076
  200.4 45.9 %reduce-scatter.7.cloned.1.call-start = ((), (), s32[]{:S(2)}) async-start(), calls=%async_computation.10 | async-start | bytes 655360 | tf_op jit(solution)/shard_map/reduce_scatter | solution.py:50
  250.8 137.0 %all-to-all-start.3 = ((bf16[32,256,256]{2,1,0:T(8,128)(2,1)}), bf16[32,256,256]{2,1,0:T(8,128)(2,1)}, u32[]{:S(2)}, u32[]{:S(2)}) async-start(bf16[32,256,256]{2,1,0:T(8,128)(2,1)} %stack.5), calls=%async_computation.5 | async-start | bytes 8388608 | tf_op jit(solution)/shard_map/all_to_all | solution.py:66
  259.0 78.8 %all-gather.7.cloned.1.call-start = ((), (), s32[]{:S(2)}) async-start(), calls=%async_computation.11 | async-start | bytes 1572864 | tf_op jit(solution)/shard_map/all_gather | solution.py:21
  387.8 317.3 %all-to-all-start.2 = ((bf16[32,256,256]{2,1,0:T(8,128)(2,1)}), bf16[32,256,256]{2,1,0:T(8,128)(2,1)}, u32[]{:S(2)}, u32[]{:S(2)}) async-start(bf16[32,256,256]{2,1,0:T(8,128)(2,1)} %convert_element_type.81), calls=%async_computation.4 | async-start | bytes 8388608 | tf_op jit(solution)/shard_map/all_to_all | solution.py:40
  396.1 50.4 %reduce-scatter.9.cloned.1.call-start = ((), (), s32[]{:S(2)}) async-start(), calls=%async_computation.12 | async-start | bytes 1572864 | tf_op jit(solution)/shard_map/reduce_scatter | solution.py:50
  430.6 1.3 copy-start.3
  430.7 304.1 %copy-start.1 = (bf16[256,256]{1,0:T(8,128)(2,1)S(1)}, bf16[256,256]{1,0:T(8,128)(2,1)}, u32[]{:S(2)}) copy-start(bf16[256,256]{1,0:T(8,128)(2,1)} %param.11) | copy-start | bytes 393220
  431.8 272.1 %all-reduce.4.cloned.1.call-start = ((), (), s32[]{:S(2)}) async-start(), calls=%async_computation.14 | async-start | bytes 524288
  432.8 300.4 %reduce-scatter.11.cloned.1.call-start = ((), (), s32[]{:S(2)}) async-start(), calls=%async_computation.13 | async-start | bytes 655360 | tf_op jit(solution)/shard_map/reduce_scatter | solution.py:50
Sparse Core Ops, SparseCore 0:
  96.9 9.3 all-gather.4
  200.5 14.5 reduce-scatter.4
  217.8 28.4 reduce-scatter.6
  325.2 12.5 all-gather.6
  431.9 14.5 reduce-scatter.8
  451.8 252.0 all-reduce.3
  706.4 26.7 reduce-scatter.10
